TPU v7x, 32 devices: a whole 2x2x4 slice. The times are simulated.
32 devices in a mesh: space: 16 (over z, y, core), slab: 2 (over x).
Axes of the slice: x: 2, y: 2, z: 4, core: 2. Of those that a mesh axis runs over, the one named last changes fastest.
Arguments:
- wavefunctions: bfloat16 [64, 83232], P(None, ('space', 'slab')), may hold values from -6 to 6
- kinetic: bfloat16 [729, 729], replicated, may hold values from -1 to 2, as said below
- cell_scale: float32 [128], P(('space', 'slab')), may hold values from 0.5 to 2
- potential: float32 [128, 729], P(('space', 'slab')), may hold values from -1 to 1
- cell_nodes: int32 [128, 729], P(('space', 'slab')), may hold values from 0 to 2600, as said below
- face_space: int32 [64, 289], P(('space', 'slab')), may hold values from 0 to 2600, as said below
- face_slab: int32 [64, 153], P(('space', 'slab')), may hold values from 0 to 2600, as said below
- projectors: bfloat16 [128, 18, 729], P(('space', 'slab')), may hold values from -0.21875 to 0.21875
- cell_atom: int32 [128], P(('space', 'slab')), may hold values from 0 to 7
- coupling: float32 [128, 18, 18], P(('space', 'slab')), may hold values from -8 to 8
Outputs:
- filtered: float32 [64, 83232], P(None, ('space', 'slab'))
Inputs may be any that keep to these rules, and one draw needn't show every extreme that they name: `cell_nodes`: each block's 4 cells tile a block of 1 x 2 x 2 cells of degree 8; within a block the cell nodes name the nodes of that block's node grid, numbered in an order of the block's own. `face_space`: row 2b lists the nodes of block b's lower face across the long direction and row 2b + 1 those of its upper face, both in one fixed order of the face's positions, so that a block's upper face and the next block's lower face list the same nodes at equal positions; each row names distinct nodes. `face_slab`: likewise for the faces across the cross-section between blocks l and l + 1 of a row. `kinetic`: A symmetric matrix.
All inputs are finite; a program needn't handle non-finite values.
Results may differ from a plain program's by a relative error of at most 0.0039.
Values may be sent and summed in bfloat16 or wider, within the bound.
A program may use at most 64 MiB of HBM per device.

v0:
```python
import jax
import jax.numpy as jnp
from jax import lax
from jax.sharding import PartitionSpec as P

filter_centre = 8.0
filter_half = 8.0


def extended(block, sides, width):
    for axis, dim in sides:
        count = lax.axis_size(axis)
        forward = [(i, i + 1) for i in range(count - 1)]
        backward = [(target, source) for source, target in forward]
        low = lax.ppermute(
            lax.slice_in_dim(block, block.shape[dim] - width, None, axis=dim), axis, forward
        )
        high = lax.ppermute(lax.slice_in_dim(block, 0, width, axis=dim), axis, backward)
        block = jnp.concatenate([low, block, high], axis=dim)
    return block


def space_sum(assembled, face_space):
    lower_idx = face_space[0]
    upper_idx = face_space[1]
    face_width = lower_idx.shape[0]
    outgoing = jnp.concatenate(
        [jnp.take(assembled, lower_idx, axis=1), jnp.take(assembled, upper_idx, axis=1)], axis=1
    )
    padded = extended(outgoing, (("space", 1),), face_width)
    from_below = padded[:, :face_width]
    from_above = padded[:, 3 * face_width :]
    return assembled.at[:, lower_idx].add(from_below).at[:, upper_idx].add(from_above)


def slab_sum(assembled, face_slab):
    lower_idx = face_slab[0]
    upper_idx = face_slab[1]
    face_width = lower_idx.shape[0]
    outgoing = jnp.concatenate(
        [jnp.take(assembled, lower_idx, axis=1), jnp.take(assembled, upper_idx, axis=1)], axis=1
    )
    padded = extended(outgoing, (("slab", 1),), face_width)
    from_below = padded[:, :face_width]
    from_above = padded[:, 3 * face_width :]
    return assembled.at[:, lower_idx].add(from_below).at[:, upper_idx].add(from_above)


def shards(
    wavefunctions,
    kinetic,
    cell_scale,
    potential,
    cell_nodes,
    face_space,
    face_slab,
    projectors,
    cell_atom,
    coupling,
):
    width = wavefunctions.shape[0]
    node_count = wavefunctions.shape[1]
    cell_count = cell_scale.shape[0]
    order = kinetic.shape[0]
    atom_slots = coupling.shape[0]
    proj_count = coupling.shape[1]
    slab_count = lax.axis_size("slab")
    index_flat = cell_nodes.reshape(-1)
    onehot = (
        cell_atom[:, None] == jnp.arange(slab_count * atom_slots, dtype=jnp.int32)[None, :]
    ).astype(jnp.float32)
    onehot_half = onehot.astype(jnp.bfloat16)

    def operate(field_now):
        values = jnp.take(field_now.astype(jnp.bfloat16), index_flat, axis=1).reshape(
            width, cell_count, order
        )
        margin = jnp.einsum("wcj,cpj->cpw", values, projectors, preferred_element_type=jnp.float32)
        partial_value = jnp.einsum("ca,cpw->apw", onehot, margin, precision=lax.Precision.HIGHEST)
        outgoing = partial_value.reshape(slab_count, atom_slots, proj_count * width)
        arrived = lax.all_to_all(outgoing, "slab", split_axis=0, concat_axis=0, tiled=True)
        summed = jnp.sum(arrived, axis=0).reshape(atom_slots, proj_count, width)
        coupled = jnp.einsum(
            "aqp,apw->aqw", coupling, summed, precision=lax.Precision.HIGHEST
        ).astype(jnp.bfloat16)
        coupled_row = lax.all_gather(
            coupled.reshape(atom_slots, proj_count * width), "slab", axis=0, tiled=True
        )
        per_cell = jnp.dot(onehot_half, coupled_row, preferred_element_type=jnp.float32).astype(
            jnp.bfloat16
        )
        per_cell = per_cell.reshape(cell_count, proj_count, width)
        nonlocal_part = jnp.einsum(
            "cpw,cpj->wcj", per_cell, projectors, preferred_element_type=jnp.float32
        )
        kinetic_part = jnp.dot(
            values.reshape(width * cell_count, order), kinetic, preferred_element_type=jnp.float32
        )
        kinetic_part = kinetic_part.reshape(width, cell_count, order)
        total = (
            cell_scale[None, :, None] * kinetic_part
            + potential[None] * values.astype(jnp.float32)
            + nonlocal_part
        )
        assembled = (
            jnp.zeros((width, node_count), jnp.float32)
            .at[:, index_flat]
            .add(total.reshape(width, cell_count * order))
        )
        assembled = space_sum(assembled, face_space)
        assembled = slab_sum(assembled, face_slab)
        return assembled

    start = wavefunctions.astype(jnp.float32)
    current = (operate(start) - filter_centre * start) / filter_half
    following = 2.0 * (operate(current) - filter_centre * current) / filter_half - start
    return following


def solution(mesh):
    placed = (
        P(None, ("space", "slab")),
        P(),
        P(("space", "slab")),
        P(("space", "slab"), None),
        P(("space", "slab"), None),
        P(("space", "slab"), None),
        P(("space", "slab"), None),
        P(("space", "slab"), None, None),
        P(("space", "slab")),
        P(("space", "slab"), None, None),
    )
    return jax.shard_map(
        shards, mesh=mesh, in_specs=placed, out_specs=P(None, ("space", "slab")), check_vma=False
    )
```

profile of v0, /device:TPU:21, one launch (start us, length us, event | category | flops | bytes accessed | tf_op | source)
XLA Modules:
  0.0 150.5 jit_solution(7558636211429083473)
XLA Ops:
  2.2 6.2 %gather_fusion = bf16[2916,64]{1,0:T(8,128)(2,1)S(1)} fusion(bf16[64,2601]{0,1:T(8,128)(2,1)S(1)} %copy.62, s32[3072]{0:T(1024)S(1)} %pad_clamp_fusion), kind=kCustom, calls=%fused_computation.clone | custom fusion | bytes 758160 | tf_op jit(solution)/shard_map/jit(_take)/gather | solution.py:75
  11.7 3.3 %all-to-all-start = ((f32[2,4,1152]{2,1,0:T(4,128)}), f32[2,4,1152]{2,1,0:T(4,128)S(1)}, u32[]{:S(2)}, u32[]{:S(2)}) async-start(f32[2,4,1152]{2,1,0:T(4,128)} %reshape.203), calls=%async_computation | async-start | bytes 73728 | tf_op jit(solution)/shard_map/all_to_all | solution.py:81
  15.6 2.1 %all-to-all-done = f32[2,4,1152]{2,1,0:T(4,128)S(1)} async-done(((f32[2,4,1152]{2,1,0:T(4,128)}), f32[2,4,1152]{2,1,0:T(4,128)S(1)}, u32[]{:S(2)}, u32[]{:S(2)}) %all-to-all-start) | async-done | bytes 36896 | tf_op jit(solution)/shard_map/all_to_all | solution.py:81
  18.2 3.2 %all-gather = bf16[2,4,1152]{2,1,0:T(4,128)(2,1)S(1)} all-gather(bf16[1,4,1152]{2,1,0:T(4,128)(2,1)S(1)} %reshape.383), channel_id=1, replica_groups=mesh['space'=16,'slab'=2] {'slab'}, dimensions={0}, use_global_device_ids=true | all-gather | bytes 27648 | tf_op jit(solution)/shard_map/all_gather | solution.py:86
  25.2 17.6 %scatter_custom_fusion = f32[64,2601]{0,1:T(8,128)S(1)} fusion(s32[2916]{0:T(1024)S(1)} %fusion.39, f32[2916,64]{1,0:T(8,128)} %copy.73, f32[]{:T(128)} %constant.11.clone.1), kind=kCustom, calls=%fused_computation.46 | custom fusion | flops 186624 | bytes 666368 | tf_op jit(solution)/shard_map/scatter-add | solution.py:108
  45.1 6.0 %collective-permute-start = (f32[64,289]{0,1:T(8,128)S(1)}, f32[64,289]{0,1:T(8,128)S(1)}, u32[]{:S(2)}, u32[]{:S(2)}) collective-permute-start(f32[64,289]{0,1:T(8,128)S(1)} %select_bitcast_fusion.5), channel_id=1, source_target_pairs={{0,2},{2,4},{4,6},{6,8},{8,10},{10,12},{12,14},{14,16},{16,18},{18... | collective-permute-start | bytes 221960 | tf_op jit(solution)/shard_map/ppermute | solution.py:15
  51.3 1.9 %collective-permute-start.1 = (f32[64,289]{0,1:T(8,128)S(1)}, f32[64,289]{0,1:T(8,128)S(1)}, u32[]{:S(2)}, u32[]{:S(2)}) collective-permute-start(f32[64,289]{0,1:T(8,128)S(1)} %select_bitcast_fusion.4), channel_id=1, source_target_pairs={{2,0},{4,2},{6,4},{8,6},{10,8},{12,10},{14,12},{16,14},{18,16},{20... | collective-permute-start | bytes 221960 | tf_op jit(solution)/shard_map/ppermute | solution.py:18
  53.3 2.6 %scatter_custom_fusion.1 = f32[64,2601]{0,1:T(8,128)S(1)} fusion(f32[64,2601]{0,1:T(8,128)S(1)} %scatter_custom_fusion, s32[289]{0:T(512)S(1)} %get-tuple-element.11, f32[64,289]{0,1:T(8,128)S(1)} %collective-permute-done), kind=kCustom, calls=%fused_computation.54 | custom fusion | flops 18496 | bytes 817408 | tf_op jit(solution)/shard_map/scatter-add | solution.py:33
  55.9 2.8 %collective-permute-done.1 = f32[64,289]{0,1:T(8,128)S(1)} collective-permute-done((f32[64,289]{0,1:T(8,128)S(1)}, f32[64,289]{0,1:T(8,128)S(1)}, u32[]{:S(2)}, u32[]{:S(2)}) %collective-permute-start.1) | collective-permute-done | bytes 74016 | tf_op jit(solution)/shard_map/ppermute | solution.py:18
  58.7 2.6 %scatter_custom_fusion.2 = f32[64,2601]{0,1:T(8,128)S(1)} fusion(f32[64,2601]{0,1:T(8,128)S(1)} %scatter_custom_fusion.1, s32[289]{0:T(512)S(1)} %get-tuple-element.10, f32[64,289]{0,1:T(8,128)S(1)} %collective-permute-done.1), kind=kCustom, calls=%fused_computation.52 | custom fusion | flops 18496 | bytes 817408 | tf_op jit(solution)/shard_map/scatter-add | solution.py:33
  65.8 2.0 %scatter_custom_fusion.3 = f32[64,2601]{0,1:T(8,128)S(1)} fusion(f32[64,2601]{0,1:T(8,128)S(1)} %scatter_custom_fusion.2, s32[153]{0:T(256)S(1)} %bitcast.101, f32[64,153]{0,1:T(8,128)S(1)} %collective-permute-done.2), kind=kCustom, calls=%fused_computation.70 | custom fusion | flops 9792 | bytes 747776 | tf_op jit(solution)/shard_map/scatter-add | solution.py:46
  67.9 2.0 %collective-permute-done.3 = f32[64,153]{0,1:T(8,128)S(1)} collective-permute-done((f32[64,153]{0,1:T(8,128)S(1)}, f32[64,153]{0,1:T(8,128)S(1)}, u32[]{:S(2)}, u32[]{:S(2)}) %collective-permute-start.3) | collective-permute-done | bytes 39200 | tf_op jit(solution)/shard_map/ppermute | solution.py:18
  73.5 7.1 %gather_fusion.5 = bf16[2916,64]{1,0:T(8,128)(2,1)} fusion(bf16[64,2601]{0,1:T(8,128)(2,1)S(1)} %copy.75, s32[3072]{0:T(1024)S(1)} %pad_clamp_fusion), kind=kCustom, calls=%fused_computation.3.clone | custom fusion | bytes 758160 | tf_op jit(solution)/shard_map/jit(_take)/gather | solution.py:75
  80.6 2.5 %select_bitcast_fusion = bf16[64,2916]{0,1:T(8,128)(2,1)S(1)} fusion(bf16[2916,64]{1,0:T(8,128)(2,1)} %gather_fusion.5, pred[2916]{0:T(1024)(128)(4,1)S(1)} %compare_and_fusion), kind=kLoop, calls=%fused_computation.40 | loop fusion | flops 186624 | bytes 749412 | tf_op jit(solution)/shard_map/jit(_take)/select_n | solution.py:75
  84.7 3.3 %all-to-all-start.1 = ((f32[2,4,1152]{2,1,0:T(4,128)}), f32[2,4,1152]{2,1,0:T(4,128)S(1)}, u32[]{:S(2)}, u32[]{:S(2)}) async-start(f32[2,4,1152]{2,1,0:T(4,128)} %reshape.208), calls=%async_computation.1 | async-start | bytes 73728 | tf_op jit(solution)/shard_map/all_to_all | solution.py:81
  88.2 2.5 %all-to-all-done.1 = f32[2,4,1152]{2,1,0:T(4,128)S(1)} async-done(((f32[2,4,1152]{2,1,0:T(4,128)}), f32[2,4,1152]{2,1,0:T(4,128)S(1)}, u32[]{:S(2)}, u32[]{:S(2)}) %all-to-all-start.1) | async-done | bytes 36896 | tf_op jit(solution)/shard_map/all_to_all | solution.py:81
  91.2 3.2 %all-gather.1 = bf16[2,4,1152]{2,1,0:T(4,128)(2,1)S(1)} all-gather(bf16[1,4,1152]{2,1,0:T(4,128)(2,1)S(1)} %reshape.385), channel_id=1, replica_groups=mesh['space'=16,'slab'=2] {'slab'}, dimensions={0}, use_global_device_ids=true | all-gather | bytes 27648 | tf_op jit(solution)/shard_map/all_gather | solution.py:86
  98.2 17.6 %scatter_custom_fusion.5 = f32[64,2601]{0,1:T(8,128)S(1)} fusion(s32[2916]{0:T(1024)S(1)} %fusion.39, f32[2916,64]{1,0:T(8,128)} %copy.86, f32[]{:T(128)} %constant.11.clone.1), kind=kCustom, calls=%fused_computation.44 | custom fusion | flops 186624 | bytes 666368 | tf_op jit(solution)/shard_map/scatter-add | solution.py:108
  119.5 6.1 %collective-permute-start.4 = (f32[64,289]{0,1:T(8,128)S(1)}, f32[64,289]{0,1:T(8,128)}, u32[]{:S(2)}, u32[]{:S(2)}) collective-permute-start(f32[64,289]{0,1:T(8,128)S(1)} %select_bitcast_fusion.3), channel_id=1, source_target_pairs={{0,2},{2,4},{4,6},{6,8},{8,10},{10,12},{12,14},{14,16},{16,18},{18... | collective-permute-start | bytes 221960 | tf_op jit(solution)/shard_map/ppermute | solution.py:15
  128.3 3.0 %scatter_custom_fusion.6 = f32[64,2601]{0,1:T(8,128)S(1)} fusion(f32[64,2601]{0,1:T(8,128)S(1)} %scatter_custom_fusion.5, s32[289]{0:T(512)S(1)} %get-tuple-element.11, f32[64,289]{0,1:T(8,128)} %collective-permute-done.4), kind=kCustom, calls=%fused_computation.50 | custom fusion | flops 18496 | bytes 739840 | tf_op jit(solution)/shard_map/scatter-add | solution.py:33
  131.3 2.7 %collective-permute-done.5 = f32[64,289]{0,1:T(8,128)S(1)} collective-permute-done((f32[64,289]{0,1:T(8,128)}, f32[64,289]{0,1:T(8,128)S(1)}, u32[]{:S(2)}, u32[]{:S(2)}) %collective-permute-start.5) | collective-permute-done | bytes 74016 | tf_op jit(solution)/shard_map/ppermute | solution.py:18
  134.0 2.8 %scatter_custom_fusion.7 = f32[64,2601]{0,1:T(8,128)S(1)} fusion(f32[64,2601]{0,1:T(8,128)S(1)} %scatter_custom_fusion.6, s32[289]{0:T(512)S(1)} %get-tuple-element.10, f32[64,289]{0,1:T(8,128)S(1)} %collective-permute-done.5), kind=kCustom, calls=%fused_computation.48 | custom fusion | flops 18496 | bytes 817408 | tf_op jit(solution)/shard_map/scatter-add | solution.py:33
  141.3 2.0 %scatter_custom_fusion.8 = f32[64,2601]{0,1:T(8,128)S(1)} fusion(f32[64,2601]{0,1:T(8,128)S(1)} %scatter_custom_fusion.7, s32[153]{0:T(256)} %bitcast.102, f32[64,153]{0,1:T(8,128)S(1)} %collective-permute-done.6), kind=kCustom, calls=%fused_computation.66 | custom fusion | flops 9792 | bytes 747776 | tf_op jit(solution)/shard_map/scatter-add | solution.py:46
  148.3 2.2 %convert_subtract_fusion = f32[64,2601]{1,0:T(8,128)} fusion(bf16[64,2601]{1,0:T(8,128)(2,1)} %param.16, f32[64,2601]{1,0:T(8,128)} %copy.87, f32[64,2601]{1,0:T(8,128)S(1)} %copy.74), kind=kLoop, calls=%fused_computation.38 | loop fusion | flops 998784 | bytes 2330496 | tf_op jit(solution)/shard_map/sub | solution.py:116
  (112 shorter events, 42.6 us)
Async XLA Ops:
  0.0 22.0 %copy-start = (bf16[729,729]{1,0:T(8,128)(2,1)S(1)}, bf16[729,729]{1,0:T(8,128)(2,1)}, u32[]{:S(2)}) copy-start(bf16[729,729]{1,0:T(8,128)(2,1)} %param.17) | copy-start | bytes 3188650
  8.4 1.8 %copy-start.1 = (bf16[4,18,729]{2,0,1:T(4,128)(2,1)S(1)}, bf16[4,18,729]{2,0,1:T(4,128)(2,1)}, u32[]{:S(2)}) copy-start(bf16[4,18,729]{2,0,1:T(4,128)(2,1)} %param.23) | copy-start | bytes 314932
  10.0 0.7 copy-start.7
  10.0 5.0 %copy-start.6 = (s32[2,153]{1,0:T(2,128)S(1)}, s32[2,153]{1,0:T(2,128)}, u32[]{:S(2)}) copy-start(s32[2,153]{1,0:T(2,128)} %param.22) | copy-start | bytes 3676
  10.0 5.0 %copy-start.5 = (s32[2,289]{1,0:T(2,128)S(1)}, s32[2,289]{1,0:T(2,128)}, u32[]{:S(2)}) copy-start(s32[2,289]{1,0:T(2,128)} %param.21) | copy-start | bytes 6940
  10.0 5.1 %copy-start.4 = (s32[4,729]{1,0:T(4,128)S(1)}, s32[4,729]{1,0:T(4,128)}, u32[]{:S(2)}) copy-start(s32[4,729]{1,0:T(4,128)} %param.20) | copy-start | bytes 34996
  10.3 7.6 %copy-start.2 = (f32[4,18,18]{2,0,1:T(4,128)S(1)}, f32[4,18,18]{2,0,1:T(4,128)}, u32[]{:S(2)}) copy-start(f32[4,18,18]{2,0,1:T(4,128)} %param.25) | copy-start | bytes 15556
  11.7 6.1 %all-to-all-start = ((f32[2,4,1152]{2,1,0:T(4,128)}), f32[2,4,1152]{2,1,0:T(4,128)S(1)}, u32[]{:S(2)}, u32[]{:S(2)}) async-start(f32[2,4,1152]{2,1,0:T(4,128)} %reshape.203), calls=%async_computation | async-start | bytes 73728 | tf_op jit(solution)/shard_map/all_to_all | solution.py:81
  14.9 7.1 %copy-start.3 = (f32[4,729]{1,0:T(4,128)S(1)}, f32[4,729]{1,0:T(4,128)}, u32[]{:S(2)}) copy-start(f32[4,729]{1,0:T(4,128)} %param.19) | copy-start | bytes 34996
  15.0 7.1 %copy-start.8 = (f32[4]{0:T(128)S(1)}, f32[4]{0:T(128)}, u32[]{:S(2)}) copy-start(f32[4]{0:T(128)} %param.18) | copy-start | bytes 52
  45.1 8.1 %collective-permute-start = (f32[64,289]{0,1:T(8,128)S(1)}, f32[64,289]{0,1:T(8,128)S(1)}, u32[]{:S(2)}, u32[]{:S(2)}) collective-permute-start(f32[64,289]{0,1:T(8,128)S(1)} %select_bitcast_fusion.5), channel_id=1, source_target_pairs={{0,2},{2,4},{4,6},{6,8},{8,10},{10,12},{12,14},{14,16},{16,18},{18... | collective-permute-start | bytes 221960 | tf_op jit(solution)/shard_map/ppermute | solution.py:15
  51.3 7.4 %collective-permute-start.1 = (f32[64,289]{0,1:T(8,128)S(1)}, f32[64,289]{0,1:T(8,128)S(1)}, u32[]{:S(2)}, u32[]{:S(2)}) collective-permute-start(f32[64,289]{0,1:T(8,128)S(1)} %select_bitcast_fusion.4), channel_id=1, source_target_pairs={{2,0},{4,2},{6,4},{8,6},{10,8},{12,10},{14,12},{16,14},{18,16},{20... | collective-permute-start | bytes 221960 | tf_op jit(solution)/shard_map/ppermute | solution.py:18
  62.7 3.1 %collective-permute-start.2 = (f32[64,153]{0,1:T(8,128)S(1)}, f32[64,153]{0,1:T(8,128)S(1)}, u32[]{:S(2)}, u32[]{:S(2)}) collective-permute-start(f32[64,153]{0,1:T(8,128)S(1)} %select_bitcast_fusion.9), channel_id=1, source_target_pairs={{0,1},{2,3},{4,5},{6,7},{8,9},{10,11},{12,13},{14,15},{16,17},{18,... | collective-permute-start | bytes 117512 | tf_op jit(solution)/shard_map/ppermute | solution.py:15
  64.4 5.4 %collective-permute-start.3 = (f32[64,153]{0,1:T(8,128)S(1)}, f32[64,153]{0,1:T(8,128)S(1)}, u32[]{:S(2)}, u32[]{:S(2)}) collective-permute-start(f32[64,153]{0,1:T(8,128)S(1)} %select_bitcast_fusion.8), channel_id=1, source_target_pairs={{1,0},{3,2},{5,4},{7,6},{9,8},{11,10},{13,12},{15,14},{17,16},{19,... | collective-permute-start | bytes 117512 | tf_op jit(solution)/shard_map/ppermute | solution.py:18
  65.8 5.9 %copy-start.9 = (s32[153,1]{0,1:T(1,128)}, s32[153,1]{0,1:T(1,128)S(1)}, u32[]{:S(2)}) copy-start(s32[153,1]{0,1:T(1,128)S(1)} %get-tuple-element.15) | copy-start | bytes 1840
  84.7 6.1 %all-to-all-start.1 = ((f32[2,4,1152]{2,1,0:T(4,128)}), f32[2,4,1152]{2,1,0:T(4,128)S(1)}, u32[]{:S(2)}, u32[]{:S(2)}) async-start(f32[2,4,1152]{2,1,0:T(4,128)} %reshape.208), calls=%async_computation.1 | async-start | bytes 73728 | tf_op jit(solution)/shard_map/all_to_all | solution.py:81
  119.5 8.7 %collective-permute-start.4 = (f32[64,289]{0,1:T(8,128)S(1)}, f32[64,289]{0,1:T(8,128)}, u32[]{:S(2)}, u32[]{:S(2)}) collective-permute-start(f32[64,289]{0,1:T(8,128)S(1)} %select_bitcast_fusion.3), channel_id=1, source_target_pairs={{0,2},{2,4},{4,6},{6,8},{8,10},{10,12},{12,14},{14,16},{16,18},{18... | collective-permute-start | bytes 221960 | tf_op jit(solution)/shard_map/ppermute | solution.py:15
  126.3 7.6 %collective-permute-start.5 = (f32[64,289]{0,1:T(8,128)}, f32[64,289]{0,1:T(8,128)S(1)}, u32[]{:S(2)}, u32[]{:S(2)}) collective-permute-start(f32[64,289]{0,1:T(8,128)} %select_bitcast_fusion.2), channel_id=1, source_target_pairs={{2,0},{4,2},{6,4},{8,6},{10,8},{12,10},{14,12},{16,14},{18,16},{20... | collective-permute-start | bytes 221960 | tf_op jit(solution)/shard_map/ppermute | solution.py:18
  138.2 3.1 %collective-permute-start.6 = (f32[64,153]{0,1:T(8,128)S(1)}, f32[64,153]{0,1:T(8,128)S(1)}, u32[]{:S(2)}, u32[]{:S(2)}) collective-permute-start(f32[64,153]{0,1:T(8,128)S(1)} %select_bitcast_fusion.7), channel_id=1, source_target_pairs={{0,1},{2,3},{4,5},{6,7},{8,9},{10,11},{12,13},{14,15},{16,17},{18,... | collective-permute-start | bytes 117512 | tf_op jit(solution)/shard_map/ppermute | solution.py:15
  140.0 5.2 %collective-permute-start.7 = (f32[64,153]{0,1:T(8,128)S(1)}, f32[64,153]{0,1:T(8,128)S(1)}, u32[]{:S(2)}, u32[]{:S(2)}) collective-permute-start(f32[64,153]{0,1:T(8,128)S(1)} %select_bitcast_fusion.6), channel_id=1, source_target_pairs={{1,0},{3,2},{5,4},{7,6},{9,8},{11,10},{13,12},{15,14},{17,16},{19,... | collective-permute-start | bytes 117512 | tf_op jit(solution)/shard_map/ppermute | solution.py:18
where the time goes:
time: 151 us; the launch traced here: 150 us
  other arithmetic  63.8 us (42%)
  local copies, waits for them, and re-layouts  33.5 us (22%)
  starting transfers between devices  28.3 us (19%)
  waiting for transfers between devices  14.1 us (9%)
  blocking collectives  6.43 us (4%)
  matrix products  3.66 us (2%)
    scatter-add x2, other arithmetic, operate(): assembled = jnp.zeros((width, node_count), jnp.float32).at[:, index_flat]...  35.2 us
    ppermute x4, starting transfers between devices, extended(): lax.ppermute(lax.slice_in_dim(block, block.shape[dim] - width, None, axis...  15.3 us
    gather x2, local copies, waits for them, and re-layouts, operate(): jnp.take(field_now.astype(jnp.bfloat16), index_flat, axis=1)  13.2 us
    scatter-add x4, other arithmetic, space_sum(): assembled.at[:, lower_idx].add(from_below).at[:, upper_idx].add(from_above)  11 us
    ppermute x4, waiting for transfers between devices, extended(): lax.ppermute(lax.slice_in_dim(block, 0, width, axis=dim), axis, backward)  9.27 us
    scatter-add x4, other arithmetic, slab_sum(): assembled.at[:, lower_idx].add(from_below).at[:, upper_idx].add(from_above)  7.76 us
    all_to_all x2, starting transfers between devices, operate(): lax.all_to_all(outgoing, 'slab', split_axis=0, concat_axis=0, tiled=True)  6.52 us
    all_gather x2, blocking collectives, operate(): lax.all_gather(coupled.reshape(atom_slots, proj_count * width), 'slab', a...  6.43 us
  transfers between devices with their start and end apart: 10, of which 8 were waited for; matrix products, arithmetic and copies ran while one was open for 8% of the time, Pallas kernels for 0%

commit v1 on v0

v1 whole, which is shorter than its diff:
```python
import functools

import jax
import jax.numpy as jnp
from jax import lax
from jax.experimental import pallas as pl
from jax.experimental.pallas import tpu as pltpu
from jax.sharding import PartitionSpec as P

filter_centre = 8.0
filter_half = 8.0
BLK = 256
MESH = pl.DeviceIdType.MESH
NT = (((1,), (1,)), ((), ()))
f32 = jnp.float32
bf16 = jnp.bfloat16


def up(value, unit):
    return -(-value // unit) * unit


def kernel(
    dims,
    y_ref,
    kin_ref,
    scale_ref,
    pot_ref,
    cn_ref,
    fs_ref,
    fl_ref,
    pr_ref,
    pack_ref,
    out_ref,
    hot,
    idx,
    kin,
    pp,
    pot,
    cross,
    packs,
    coup,
    yb,
    vals,
    tot,
    asm,
    asmb,
    asm2,
    outg,
    in_space,
    in_slab,
    inc,
    marg,
    pack_send,
    pack_recv,
    marg_send,
    marg_recv,
    face_send,
    face_recv,
):
    n_space, n_slab = dims["n_space"], dims["n_slab"]
    width, nodes, cells, order = dims["width"], dims["nodes"], dims["cells"], dims["order"]
    atoms, nproj, pstride = dims["atoms"], dims["nproj"], dims["pstride"]
    fs, fl = dims["fs"], dims["fl"]
    op, npad = up(order, BLK), up(nodes, BLK)
    fsp, flp = up(fs, 128), up(fl, 128)
    jp = cells * op
    fp = up(2 * fsp + 2 * flp, BLK)
    lp = cells * pstride
    o_sl = 2 * fsp

    s = lax.axis_index("space")
    l = lax.axis_index("slab")
    above, below = lax.rem(s + 1, n_space), lax.rem(s + n_space - 1, n_space)
    right, left = lax.rem(l + 1, n_slab), lax.rem(l + n_slab - 1, n_slab)

    barrier = pltpu.get_barrier_semaphore()
    for d in range(1, n_slab):
        pl.semaphore_signal(
            barrier, inc=1, device_id={"slab": lax.rem(l + d, n_slab)}, device_id_type=MESH
        )
    for t in (above, below):
        pl.semaphore_signal(barrier, inc=1, device_id={"space": t}, device_id_type=MESH)
    pl.semaphore_wait(barrier, n_slab + 1)

    pack_copies = []
    for d in range(1, n_slab):
        copy = pltpu.make_async_remote_copy(
            src_ref=pack_ref,
            dst_ref=packs.at[d - 1],
            send_sem=pack_send.at[d - 1],
            recv_sem=pack_recv.at[d - 1],
            device_id={"slab": lax.rem(l + d, n_slab)},
            device_id_type=MESH,
        )
        copy.start()
        pack_copies.append(copy)

    idx[...] = jnp.full(idx.shape, -1, jnp.int32)
    for c in range(cells):
        idx[0:1, c * op : c * op + order] = cn_ref[c : c + 1, :]
    for k in range(2):
        idx[0:1, jp + k * fsp : jp + k * fsp + fs] = fs_ref[k : k + 1, :]
        off = jp + o_sl + k * flp
        idx[0:1, off : off + fl] = fl_ref[k : k + 1, :]

    kin[...] = jnp.zeros(kin.shape, bf16)
    kin[0:order, 0:order] = kin_ref[...]
    pp[...] = jnp.zeros(pp.shape, bf16)
    pot[...] = jnp.zeros(pot.shape, f32)
    pot[0:cells, 0:order] = pot_ref[...]
    yb[...] = jnp.zeros(yb.shape, bf16)
    yb[:, 0:nodes] = y_ref[...]
    for c in range(cells):
        pp[c * pstride : c * pstride + nproj, c * op : c * op + order] = pr_ref[c]

    @pl.loop(0, npad // BLK)
    def _(b):
        rows = lax.broadcasted_iota(jnp.int32, (BLK, BLK), 0).astype(f32).astype(bf16)
        for j in range((jp + fp) // BLK):
            cols = slice(j * BLK, (j + 1) * BLK)
            shifted = (idx[0:1, cols] - b * BLK).astype(f32).astype(bf16)
            hit = rows == jnp.broadcast_to(shifted, (BLK, BLK))
            hot[pl.ds(pl.multiple_of(b * BLK, BLK), BLK), cols] = jnp.where(
                hit, jnp.ones((), bf16), jnp.zeros((), bf16)
            )

    slab_row = idx[0:1, jp + o_sl : jp + o_sl + 2 * flp].astype(f32)
    slab_row = jnp.where(slab_row < 0, -2.0, slab_row)
    for k in range(2 * fsp // 128):
        row = idx[0:1, jp + k * 128 : jp + (k + 1) * 128].astype(f32)
        col = jnp.broadcast_to(row, (128, 128)).T
        cross[k * 128 : (k + 1) * 128, :] = jnp.where(col[:, 0:1] == slab_row, 1.0, 0.0).astype(bf16)

    for copy in pack_copies:
        copy.wait()
    own_row = pack_ref[atoms * pstride : atoms * pstride + 1, :]
    own_col = jnp.broadcast_to(own_row, (lp, lp)).T
    chosen = jnp.zeros((lp, lp), f32)
    for d in range(n_slab):
        source = lax.rem(l + n_slab - d, n_slab)
        for i in range(atoms):
            part = slice(i * pstride, (i + 1) * pstride)
            block = pack_ref[part, :] if d == 0 else packs[d - 1, part, :]
            tiled = jnp.concatenate([block] * cells, axis=0)
            chosen += jnp.where(own_col == (source * atoms + i).astype(f32), tiled, 0.0)
    for d in range(n_slab):
        last = slice(atoms * pstride, atoms * pstride + 1)
        row = pack_ref[last, :] if d == 0 else packs[d - 1, last, :]
        coup[d] = jnp.where(own_col == row, chosen, 0.0)

    lanes = lax.broadcasted_iota(jnp.int32, (1, fp), 1)
    has_below, has_above = s > 0, s < n_space - 1
    has_left, has_right = l > 0, l < n_slab - 1
    keep = (
        ((lanes < fsp) & has_below)
        | ((lanes >= fsp) & (lanes < o_sl) & has_above)
        | ((lanes >= o_sl) & (lanes < o_sl + flp) & has_left)
        | ((lanes >= o_sl + flp) & (lanes < o_sl + 2 * flp) & has_right)
    ).astype(f32)

    inc[...] = jnp.zeros(inc.shape, bf16)

    def face_copy(step, which, src, landing, device):
        count = landing.shape[-1]
        return pltpu.make_async_remote_copy(
            src_ref=outg.at[step, :, src : src + count],
            dst_ref=landing.at[step, which % 2],
            send_sem=face_send.at[step, which],
            recv_sem=face_recv.at[step, which],
            device_id=device,
            device_id_type=MESH,
        )

    for step in range(2):
        for c in range(cells):
            @pl.loop(0, op // BLK)
            def _(j, c=c):
                at = pl.ds(pl.multiple_of(c * op + j * BLK, BLK), BLK)
                got = jnp.dot(yb[...], hot[:, at], preferred_element_type=f32)
                to = pl.ds(pl.multiple_of(j * BLK, BLK), BLK)
                vals[c * width : (c + 1) * width, to] = got.astype(bf16)

        margin = jnp.zeros((width, lp), f32)
        for c in range(cells):
            margin += lax.dot_general(
                vals[c * width : (c + 1) * width, :],
                pp[:, c * op : (c + 1) * op],
                NT,
                preferred_element_type=f32,
            )
        marg[step, 0] = margin
        marg_copies = []
        for d in range(1, n_slab):
            copy = pltpu.make_async_remote_copy(
                src_ref=marg.at[step, 0],
                dst_ref=marg.at[step, d],
                send_sem=marg_send.at[step, d - 1],
                recv_sem=marg_recv.at[step, d - 1],
                device_id={"slab": lax.rem(l + d, n_slab)},
                device_id_type=MESH,
            )
            copy.start()
            marg_copies.append(copy)

        asm_kin = jnp.dot(vals[...], kin[...], preferred_element_type=f32)
        for c in range(cells):
            v = vals[c * width : (c + 1) * width, :].astype(f32)
            asm[:, c * op : (c + 1) * op] = (
                scale_ref[c] * asm_kin[c * width : (c + 1) * width] + pot[c : c + 1, :] * v
            )
        coupled = lax.dot_general(
            margin, coup[0], NT, precision=lax.Precision.HIGHEST, preferred_element_type=f32
        )
        for d in range(1, n_slab):
            marg_copies[d - 1].wait()
            coupled += lax.dot_general(
                marg[step, d], coup[d], NT, precision=lax.Precision.HIGHEST, preferred_element_type=f32
            )
        coupled = coupled.astype(bf16)
        for c in range(cells):
            cols = slice(c * op, (c + 1) * op)
            total = asm[:, cols] + jnp.dot(coupled, pp[:, cols], preferred_element_type=f32)
            high = total.astype(bf16)
            tot[0:width, cols] = high
            tot[width:, cols] = (total - high.astype(f32)).astype(bf16)

        @pl.loop(0, npad // BLK)
        def _(b):
            at = pl.ds(pl.multiple_of(b * BLK, BLK), BLK)
            both = lax.dot_general(tot[...], hot[at, 0:jp], NT, preferred_element_type=f32)
            summed = both[0:width] + both[width:]
            asm[:, at] = summed
            asmb[:, at] = summed.astype(bf16)

        @pl.loop(0, fp // BLK)
        def _(b):
            at = pl.ds(pl.multiple_of(jp + b * BLK, BLK), BLK)
            to = pl.ds(pl.multiple_of(b * BLK, BLK), BLK)
            got = jnp.dot(asmb[...], hot[:, at], preferred_element_type=f32)
            outg[step, :, to] = got.astype(bf16)

        space_copies = [
            face_copy(step, 0, fsp, in_space, {"space": above}),
            face_copy(step, 1, 0, in_space, {"space": below}),
        ]
        for copy in space_copies:
            copy.start()
        for k, copy in enumerate(space_copies):
            copy.wait()
            part = slice(k * fsp, (k + 1) * fsp)
            inc[:, part] = (in_space[step, k].astype(f32) * keep[:, part]).astype(bf16)
        extra = jnp.dot(inc[:, 0:o_sl], cross[...], preferred_element_type=f32)
        part = slice(o_sl, o_sl + 2 * flp)
        outg[step, :, part] = (outg[step, :, part].astype(f32) + extra).astype(bf16)
        slab_copies = [
            face_copy(step, 2, o_sl + flp, in_slab, {"slab": right}),
            face_copy(step, 3, o_sl, in_slab, {"slab": left}),
        ]
        for copy in slab_copies:
            copy.start()
        for k, copy in enumerate(slab_copies):
            copy.wait()
            part = slice(o_sl + k * flp, o_sl + (k + 1) * flp)
            inc[:, part] = (in_slab[step, k].astype(f32) * keep[:, part]).astype(bf16)

        if step == 0:
            @pl.loop(0, npad // BLK)
            def _(b):
                at = pl.ds(pl.multiple_of(b * BLK, BLK), BLK)
                added = lax.dot_general(
                    inc[...], hot[at, jp : jp + fp], NT, preferred_element_type=f32
                )
                start = yb[:, at].astype(f32)
                current = (asm[:, at] + added - filter_centre * start) / filter_half
                asm2[:, at] = -2.0 * filter_centre * current / filter_half - start
                yb[:, at] = current.astype(bf16)
        else:
            def final(at):
                added = lax.dot_general(
                    inc[...], hot[at, jp : jp + fp], NT, preferred_element_type=f32
                )
                return 2.0 * (asm[:, at] + added) / filter_half + asm2[:, at]

            @pl.loop(0, nodes // BLK)
            def _(b):
                at = pl.ds(pl.multiple_of(b * BLK, BLK), BLK)
                out_ref[:, at] = final(at)

            if nodes % BLK:
                low = nodes // BLK * BLK
                out_ref[:, low:nodes] = final(slice(low, low + BLK))[:, 0 : nodes - low]


def shards(
    wavefunctions,
    kinetic,
    cell_scale,
    potential,
    cell_nodes,
    face_space,
    face_slab,
    projectors,
    cell_atom,
    coupling,
):
    width, nodes = wavefunctions.shape
    cells, order = cell_nodes.shape
    atoms, nproj = coupling.shape[0], coupling.shape[1]
    n_space, n_slab = lax.axis_size("space"), lax.axis_size("slab")
    fs, fl = face_space.shape[1], face_slab.shape[1]
    pstride = up(nproj, 16)
    while cells * pstride % 128:
        pstride += 16
    dims = dict(
        n_space=n_space, n_slab=n_slab, width=width, nodes=nodes, cells=cells, order=order,
        atoms=atoms, nproj=nproj, pstride=pstride, fs=fs, fl=fl,
    )
    op, npad = up(order, BLK), up(nodes, BLK)
    fsp, flp = up(fs, 128), up(fl, 128)
    jp = cells * op
    fp = up(2 * fsp + 2 * flp, BLK)
    lp = cells * pstride
    extra = pstride - nproj
    padded = jnp.pad(coupling, ((0, 0), (0, extra), (0, extra)))
    tiled = jnp.tile(padded, (1, 1, cells)).reshape(atoms * pstride, lp)
    atom_row = jnp.repeat(cell_atom.astype(f32), pstride)
    pack = jnp.concatenate([tiled, jnp.broadcast_to(atom_row[None], (8, lp))], axis=0)
    others = max(n_slab - 1, 1)
    vmem = pl.BlockSpec(memory_space=pltpu.VMEM)
    smem = pl.BlockSpec(memory_space=pltpu.SMEM)
    dma = pltpu.SemaphoreType.DMA
    return pl.pallas_call(
        functools.partial(kernel, dims),
        out_shape=jax.ShapeDtypeStruct((width, nodes), f32),
        in_specs=[vmem, vmem, smem] + [vmem] * 6,
        out_specs=vmem,
        scratch_shapes=[
            pltpu.VMEM((npad, jp + fp), bf16),
            pltpu.VMEM((8, jp + fp), jnp.int32),
            pltpu.VMEM((op, op), bf16),
            pltpu.VMEM((lp, jp), bf16),
            pltpu.VMEM((up(cells, 8), op), f32),
            pltpu.VMEM((2 * fsp, 2 * flp), bf16),
            pltpu.VMEM((others, atoms * pstride + 8, lp), f32),
            pltpu.VMEM((n_slab, lp, lp), f32),
            pltpu.VMEM((width, npad), bf16),
            pltpu.VMEM((cells * width, op), bf16),
            pltpu.VMEM((2 * width, jp), bf16),
            pltpu.VMEM((width, max(jp, npad)), f32),
            pltpu.VMEM((width, npad), bf16),
            pltpu.VMEM((width, npad), f32),
            pltpu.VMEM((2, width, fp), bf16),
            pltpu.VMEM((2, 2, width, fsp), bf16),
            pltpu.VMEM((2, 2, width, flp), bf16),
            pltpu.VMEM((width, fp), bf16),
            pltpu.VMEM((2, n_slab, width, lp), f32),
            dma((others,)),
            dma((others,)),
            dma((2, others)),
            dma((2, others)),
            dma((2, 4)),
            dma((2, 4)),
        ],
        compiler_params=pltpu.CompilerParams(
            collective_id=0, has_side_effects=True, vmem_limit_bytes=60 * 1024 * 1024
        ),
    )(
        wavefunctions, kinetic, cell_scale, potential, cell_nodes, face_space, face_slab,
        projectors, pack,
    )


def solution(mesh):
    placed = (
        P(None, ("space", "slab")),
        P(),
        P(("space", "slab")),
        P(("space", "slab"), None),
        P(("space", "slab"), None),
        P(("space", "slab"), None),
        P(("space", "slab"), None),
        P(("space", "slab"), None, None),
        P(("space", "slab")),
        P(("space", "slab"), None, None),
    )
    return jax.shard_map(
        shards, mesh=mesh, in_specs=placed, out_specs=P(None, ("space", "slab")), check_vma=False
    )
```

time: 151 us -> 74.9 us (0.50)
  the two profiles are of different devices: /device:TPU:21 before, /device:TPU:0 now
where the time goes in v1:
time: 74.9 us; the launch traced here: 74.7 us
  Pallas kernels  68.6 us (92%)
  local copies, waits for them, and re-layouts  4.72 us (6%)
  other arithmetic  1.29 us (2%)
    pallas_call x1, Pallas kernels, shards(): pl.pallas_call(functools.partial(kernel, dims), out_shape=jax.ShapeDtypeS...  68.6 us
    unnamed x3, local copies, waits for them, and re-layouts  4.34 us

profile of v1, /device:TPU:0, one launch (start us, length us, event | category | flops | bytes accessed | tf_op | source)
XLA Modules:
  0.0 74.7 jit_solution(15674647503467813616)
XLA Ops:
  0.0 0.7 convert_element_type.5
  0.7 0.1 broadcast_in_dim.10
  0.7 0.1 broadcast_in_dim.11
  0.8 0.8 %copy.13 = f32[4,18,18]{2,1,0:T(8,128)S(1)} copy(f32[4,18,18]{2,0,1:T(4,128)} %param.19) | data formatting | bytes 10368
  1.6 1.6 %copy.12.pr_ref = bf16[4,18,729]{2,1,0:T(8,128)(2,1)} copy(bf16[4,18,729]{2,0,1:T(4,128)(2,1)} %param.17) | data formatting | bytes 209952 | tf_op args[7]
  3.2 0.2 tile.9
  3.4 0.6 pad_maximum_fusion.pack_ref
  4.0 68.6 %shard_map.100 = f32[64,2601]{1,0:T(8,128)} custom-call(bf16[64,2601]{1,0:T(8,128)(2,1)} %y_ref.1, bf16[729,729]{1,0:T(8,128)(2,1)} %kin_ref.1, f32[4]{0:T(128)} %scale_ref.1, f32[4,729]{1,0:T(4,128)} %pot_ref.1, s32[4,729]{1,0:T(4,128)} %cn_ref.1, s32[2,289]{1,0:T(2,128)} %fs_ref.1, s32[2,153]{1,0:T(2,128)} %fl_ref.1, bf16[4,18,729]{2,1,0:T(8,128)(2,1)} %copy.12.pr_ref, ...), custom_call_target="tpu_custom_call" | custom-call | tf_op jit(solution)/shard_map/pallas_call | solution.py:333
  72.7 2.0 %copy.15 = f32[64,2601]{1,0:T(8,128)} copy(f32[64,2601]{1,0:T(8,128)} %shard_map.100) | data formatting | bytes 1331712
  (3 shorter events, 0.1 us)

commit v2 on v1

--- a/solution.py
+++ b/solution.py
@@ -30,9 +30,12 @@
     fs_ref,
     fl_ref,
     pr_ref,
-    pack_ref,
+    atom_ref,
+    coupling_ref,
     out_ref,
     hot,
+    hotf,
+    pack,
     idx,
     kin,
     pp,
@@ -74,6 +77,21 @@
     above, below = lax.rem(s + 1, n_space), lax.rem(s + n_space - 1, n_space)
     right, left = lax.rem(l + 1, n_slab), lax.rem(l + n_slab - 1, n_slab)
 
+    lane_cell = lax.broadcasted_iota(jnp.int32, (8, lp), 1) // pstride
+    atom_row = jnp.zeros((8, lp), f32)
+    for c in range(cells):
+        atom_row = jnp.where(lane_cell == c, atom_ref[c].astype(f32), atom_row)
+    pack[...] = jnp.zeros(pack.shape, f32)
+    for i in range(atoms):
+        part = slice(i * pstride, (i + 1) * pstride)
+        pack[i * pstride : i * pstride + nproj, 0:nproj] = coupling_ref[:, i, :]
+        once = pack[part, :]
+        many = once
+        for c in range(1, cells):
+            many = many + pltpu.roll(once, c * pstride, 1)
+        pack[part, :] = many
+    pack[atoms * pstride :, :] = atom_row
+
     barrier = pltpu.get_barrier_semaphore()
     for d in range(1, n_slab):
         pl.semaphore_signal(
@@ -86,7 +104,7 @@
     pack_copies = []
     for d in range(1, n_slab):
         copy = pltpu.make_async_remote_copy(
-            src_ref=pack_ref,
+            src_ref=pack,
             dst_ref=packs.at[d - 1],
             send_sem=pack_send.at[d - 1],
             recv_sem=pack_recv.at[d - 1],
@@ -112,18 +130,30 @@
     yb[...] = jnp.zeros(yb.shape, bf16)
     yb[:, 0:nodes] = y_ref[...]
     for c in range(cells):
-        pp[c * pstride : c * pstride + nproj, c * op : c * op + order] = pr_ref[c]
-
-    @pl.loop(0, npad // BLK)
-    def _(b):
-        rows = lax.broadcasted_iota(jnp.int32, (BLK, BLK), 0).astype(f32).astype(bf16)
-        for j in range((jp + fp) // BLK):
-            cols = slice(j * BLK, (j + 1) * BLK)
-            shifted = (idx[0:1, cols] - b * BLK).astype(f32).astype(bf16)
-            hit = rows == jnp.broadcast_to(shifted, (BLK, BLK))
-            hot[pl.ds(pl.multiple_of(b * BLK, BLK), BLK), cols] = jnp.where(
-                hit, jnp.ones((), bf16), jnp.zeros((), bf16)
-            )
+        pp[c * pstride : c * pstride + nproj, c * op : c * op + order] = pr_ref[:, c, :]
+
+    rows = lax.broadcasted_iota(jnp.int32, (BLK, BLK), 0).astype(f32).astype(bf16)
+
+    def one_hot(index_row, b):
+        shifted = (index_row - b * BLK).astype(f32).astype(bf16)
+        hit = rows == jnp.broadcast_to(shifted, (BLK, BLK))
+        return jnp.where(hit, jnp.ones((), bf16), jnp.zeros((), bf16))
+
+    per_cell = op // BLK
+
+    @pl.loop(0, cells * per_cell)
+    def _(j):
+        at = pl.ds(pl.multiple_of(j * BLK, BLK), BLK)
+        index_row = idx[0:1, at]
+        got = jnp.zeros((width, BLK), f32)
+        for b in range(npad // BLK):
+            part = slice(b * BLK, (b + 1) * BLK)
+            block = one_hot(index_row, b)
+            hot[part, at] = block
+            got += jnp.dot(yb[:, part], block, preferred_element_type=f32)
+        row = pl.ds(pl.multiple_of(j // per_cell * width, width), width)
+        to = pl.ds(pl.multiple_of(j % per_cell * BLK, BLK), BLK)
+        vals[row, to] = got.astype(bf16)
 
     slab_row = idx[0:1, jp + o_sl : jp + o_sl + 2 * flp].astype(f32)
     slab_row = jnp.where(slab_row < 0, -2.0, slab_row)
@@ -134,19 +164,19 @@
 
     for copy in pack_copies:
         copy.wait()
-    own_row = pack_ref[atoms * pstride : atoms * pstride + 1, :]
+    own_row = pack[atoms * pstride : atoms * pstride + 1, :]
     own_col = jnp.broadcast_to(own_row, (lp, lp)).T
     chosen = jnp.zeros((lp, lp), f32)
     for d in range(n_slab):
         source = lax.rem(l + n_slab - d, n_slab)
         for i in range(atoms):
             part = slice(i * pstride, (i + 1) * pstride)
-            block = pack_ref[part, :] if d == 0 else packs[d - 1, part, :]
+            block = pack[part, :] if d == 0 else packs[d - 1, part, :]
             tiled = jnp.concatenate([block] * cells, axis=0)
             chosen += jnp.where(own_col == (source * atoms + i).astype(f32), tiled, 0.0)
     for d in range(n_slab):
         last = slice(atoms * pstride, atoms * pstride + 1)
-        row = pack_ref[last, :] if d == 0 else packs[d - 1, last, :]
+        row = pack[last, :] if d == 0 else packs[d - 1, last, :]
         coup[d] = jnp.where(own_col == row, chosen, 0.0)
 
     lanes = lax.broadcasted_iota(jnp.int32, (1, fp), 1)
@@ -173,13 +203,14 @@
         )
 
     for step in range(2):
-        for c in range(cells):
-            @pl.loop(0, op // BLK)
-            def _(j, c=c):
-                at = pl.ds(pl.multiple_of(c * op + j * BLK, BLK), BLK)
+        if step > 0:
+            @pl.loop(0, cells * per_cell)
+            def _(j):
+                at = pl.ds(pl.multiple_of(j * BLK, BLK), BLK)
                 got = jnp.dot(yb[...], hot[:, at], preferred_element_type=f32)
-                to = pl.ds(pl.multiple_of(j * BLK, BLK), BLK)
-                vals[c * width : (c + 1) * width, to] = got.astype(bf16)
+                row = pl.ds(pl.multiple_of(j // per_cell * width, width), width)
+                to = pl.ds(pl.multiple_of(j % per_cell * BLK, BLK), BLK)
+                vals[row, to] = got.astype(bf16)
 
         margin = jnp.zeros((width, lp), f32)
         for c in range(cells):
@@ -228,16 +259,20 @@
         @pl.loop(0, npad // BLK)
         def _(b):
             at = pl.ds(pl.multiple_of(b * BLK, BLK), BLK)
-            both = lax.dot_general(tot[...], hot[at, 0:jp], NT, preferred_element_type=f32)
+            if step == 0:
+                for j in range(fp // BLK):
+                    hotf[at, j * BLK : (j + 1) * BLK] = one_hot(
+                        idx[0:1, jp + j * BLK : jp + (j + 1) * BLK], b
+                    )
+            both = lax.dot_general(tot[...], hot[at, :], NT, preferred_element_type=f32)
             summed = both[0:width] + both[width:]
             asm[:, at] = summed
             asmb[:, at] = summed.astype(bf16)
 
         @pl.loop(0, fp // BLK)
         def _(b):
-            at = pl.ds(pl.multiple_of(jp + b * BLK, BLK), BLK)
             to = pl.ds(pl.multiple_of(b * BLK, BLK), BLK)
-            got = jnp.dot(asmb[...], hot[:, at], preferred_element_type=f32)
+            got = jnp.dot(asmb[...], hotf[:, to], preferred_element_type=f32)
             outg[step, :, to] = got.astype(bf16)
 
         space_copies = [
@@ -269,7 +304,7 @@
             def _(b):
                 at = pl.ds(pl.multiple_of(b * BLK, BLK), BLK)
                 added = lax.dot_general(
-                    inc[...], hot[at, jp : jp + fp], NT, preferred_element_type=f32
+                    inc[...], hotf[at, :], NT, preferred_element_type=f32
                 )
                 start = yb[:, at].astype(f32)
                 current = (asm[:, at] + added - filter_centre * start) / filter_half
@@ -278,7 +313,7 @@
         else:
             def final(at):
                 added = lax.dot_general(
-                    inc[...], hot[at, jp : jp + fp], NT, preferred_element_type=f32
+                    inc[...], hotf[at, :], NT, preferred_element_type=f32
                 )
                 return 2.0 * (asm[:, at] + added) / filter_half + asm2[:, at]
 
@@ -321,11 +356,6 @@
     jp = cells * op
     fp = up(2 * fsp + 2 * flp, BLK)
     lp = cells * pstride
-    extra = pstride - nproj
-    padded = jnp.pad(coupling, ((0, 0), (0, extra), (0, extra)))
-    tiled = jnp.tile(padded, (1, 1, cells)).reshape(atoms * pstride, lp)
-    atom_row = jnp.repeat(cell_atom.astype(f32), pstride)
-    pack = jnp.concatenate([tiled, jnp.broadcast_to(atom_row[None], (8, lp))], axis=0)
     others = max(n_slab - 1, 1)
     vmem = pl.BlockSpec(memory_space=pltpu.VMEM)
     smem = pl.BlockSpec(memory_space=pltpu.SMEM)
@@ -333,10 +363,12 @@
     return pl.pallas_call(
         functools.partial(kernel, dims),
         out_shape=jax.ShapeDtypeStruct((width, nodes), f32),
-        in_specs=[vmem, vmem, smem] + [vmem] * 6,
+        in_specs=[vmem, vmem, smem] + [vmem] * 5 + [smem, vmem],
         out_specs=vmem,
         scratch_shapes=[
-            pltpu.VMEM((npad, jp + fp), bf16),
+            pltpu.VMEM((npad, jp), bf16),
+            pltpu.VMEM((npad, fp), bf16),
+            pltpu.VMEM((atoms * pstride + 8, lp), f32),
             pltpu.VMEM((8, jp + fp), jnp.int32),
             pltpu.VMEM((op, op), bf16),
             pltpu.VMEM((lp, jp), bf16),
@@ -367,7 +399,7 @@
         ),
     )(
         wavefunctions, kinetic, cell_scale, potential, cell_nodes, face_space, face_slab,
-        projectors, pack,
+        projectors.transpose(1, 0, 2), cell_atom, coupling.transpose(1, 0, 2),
     )
 
 

time: 74.9 us -> 69.5 us (0.928)
  local copies, waits for them, and re-layouts: 4.72 us -> 1.99 us
  Pallas kernels: 68.6 us -> 67.3 us
  other arithmetic: 1.29 us -> 0 us
    unnamed x3 -> x1, local copies, waits for them, and re-layouts: 4.34 us -> 1.99 us
    pallas_call x1, Pallas kernels: 68.6 us -> 67.3 us  [shards(): pl.pallas_call(functools.partial(kernel, dims), out_shape=jax.ShapeDtypeS...]
where the time goes in v2:
time: 69.5 us; the launch traced here: 69.3 us
  Pallas kernels  67.3 us (97%)
  local copies, waits for them, and re-layouts  1.99 us (3%)
    pallas_call x1, Pallas kernels, shards(): pl.pallas_call(functools.partial(kernel, dims), out_shape=jax.ShapeDtypeS...  67.3 us
    unnamed x1, local copies, waits for them, and re-layouts  1.99 us

profile of v2, /device:TPU:0, one launch (start us, length us, event | category | flops | bytes accessed | tf_op | source)
XLA Modules:
  0.0 69.3 jit_solution(9054875463901707832)
XLA Ops:
  0.0 67.3 %shard_map.100 = f32[64,2601]{1,0:T(8,128)} custom-call(bf16[64,2601]{1,0:T(8,128)(2,1)} %y_ref.1, bf16[729,729]{1,0:T(8,128)(2,1)} %kin_ref.1, f32[4]{0:T(128)} %scale_ref.1, f32[4,729]{1,0:T(4,128)} %pot_ref.1, s32[4,729]{1,0:T(4,128)} %cn_ref.1, s32[2,289]{1,0:T(2,128)} %fs_ref.1, s32[2,153]{1,0:T(2,128)} %fl_ref.1, bf16[18,4,729]{2,1,0:T(4,128)(2,1)} %bitcast.2, ...), custom_call_target="tpu_custom_call" | custom-call | tf_op jit(solution)/shard_map/pallas_call | solution.py:363
  67.3 2.0 %copy.12 = f32[64,2601]{1,0:T(8,128)} copy(f32[64,2601]{1,0:T(8,128)} %shard_map.100) | data formatting | bytes 1331712

commit v3 on v2

--- a/solution.py
+++ b/solution.py
@@ -35,19 +35,21 @@
     out_ref,
     hot,
     hotf,
+    hote,
     pack,
     idx,
     kin,
     pp,
     pot,
     cross,
+    fcol,
     packs,
     coup,
     yb,
     vals,
     tot,
     asm,
-    asmb,
+    zhl,
     asm2,
     outg,
     in_space,
@@ -99,8 +101,65 @@
         )
     for t in (above, below):
         pl.semaphore_signal(barrier, inc=1, device_id={"space": t}, device_id_type=MESH)
+    idx[...] = jnp.full(idx.shape, -1, jnp.int32)
+    for c in range(cells):
+        idx[0:1, c * op : c * op + order] = cn_ref[c : c + 1, :]
+    for k in range(2):
+        idx[0:1, jp + k * fsp : jp + k * fsp + fs] = fs_ref[k : k + 1, :]
+        off = jp + o_sl + k * flp
+        idx[0:1, off : off + fl] = fl_ref[k : k + 1, :]
+
+    kin[...] = jnp.zeros(kin.shape, bf16)
+    kin[0:order, 0:order] = kin_ref[...]
+    pp[...] = jnp.zeros(pp.shape, bf16)
+    pot[...] = jnp.zeros(pot.shape, f32)
+    pot[0:cells, 0:order] = pot_ref[...]
+    yb[...] = jnp.zeros(yb.shape, bf16)
+    yb[:, 0:nodes] = y_ref[...]
+    for c in range(cells):
+        pp[c * pstride : c * pstride + nproj, c * op : c * op + order] = pr_ref[:, c, :]
+
+    rows = lax.broadcasted_iota(jnp.int32, (BLK, BLK), 0).astype(f32).astype(bf16)
+
+    def one_hot(index_row, b):
+        shifted = (index_row - b * BLK).astype(f32).astype(bf16)
+        hit = rows == jnp.broadcast_to(shifted, (BLK, BLK))
+        return jnp.where(hit, jnp.ones((), bf16), jnp.zeros((), bf16))
+
+    slab_row = idx[0:1, jp + o_sl : jp + o_sl + 2 * flp].astype(f32)
+    slab_row = jnp.where(slab_row < 0, -2.0, slab_row)
+    for k in range(fp // 128):
+        row = idx[0:1, jp + k * 128 : jp + (k + 1) * 128].astype(f32)
+        col = jnp.broadcast_to(row, (128, 128)).T
+        col = jnp.where(col < 0, -3.0, col)
+        fcol[k * 128 : (k + 1) * 128, :] = col
+        if k < 2 * fsp // 128:
+            cross[k * 128 : (k + 1) * 128, :] = jnp.where(col[:, 0:1] == slab_row, 1.0, 0.0).astype(bf16)
+
+    per_cell = op // BLK
+
+    def build_gather(j):
+        at = pl.ds(pl.multiple_of(j * BLK, BLK), BLK)
+        index_row = idx[0:1, at]
+        got = jnp.zeros((width, BLK), f32)
+        for b in range(npad // BLK):
+            part = slice(b * BLK, (b + 1) * BLK)
+            block = one_hot(index_row, b)
+            hot[part, at] = block
+            got += jnp.dot(yb[:, part], block, preferred_element_type=f32)
+        row = pl.ds(pl.multiple_of(j // per_cell * width, width), width)
+        to = pl.ds(pl.multiple_of(j % per_cell * BLK, BLK), BLK)
+        vals[row, to] = got.astype(bf16)
+        for h in range(BLK // 128):
+            lane = pl.ds(pl.multiple_of(j * BLK + h * 128, 128), 128)
+            cell_row = jnp.broadcast_to(idx[0:1, lane].astype(f32), (128, 128))
+            for k in range(fp // 128):
+                part = slice(k * 128, (k + 1) * 128)
+                hote[part, lane] = jnp.where(fcol[part, :] == cell_row, 1.0, 0.0).astype(bf16)
+
+    half = cells * per_cell // 2
+    pl.loop(0, half)(build_gather)
     pl.semaphore_wait(barrier, n_slab + 1)
-
     pack_copies = []
     for d in range(1, n_slab):
         copy = pltpu.make_async_remote_copy(
@@ -114,53 +173,7 @@
         copy.start()
         pack_copies.append(copy)
 
-    idx[...] = jnp.full(idx.shape, -1, jnp.int32)
-    for c in range(cells):
-        idx[0:1, c * op : c * op + order] = cn_ref[c : c + 1, :]
-    for k in range(2):
-        idx[0:1, jp + k * fsp : jp + k * fsp + fs] = fs_ref[k : k + 1, :]
-        off = jp + o_sl + k * flp
-        idx[0:1, off : off + fl] = fl_ref[k : k + 1, :]
-
-    kin[...] = jnp.zeros(kin.shape, bf16)
-    kin[0:order, 0:order] = kin_ref[...]
-    pp[...] = jnp.zeros(pp.shape, bf16)
-    pot[...] = jnp.zeros(pot.shape, f32)
-    pot[0:cells, 0:order] = pot_ref[...]
-    yb[...] = jnp.zeros(yb.shape, bf16)
-    yb[:, 0:nodes] = y_ref[...]
-    for c in range(cells):
-        pp[c * pstride : c * pstride + nproj, c * op : c * op + order] = pr_ref[:, c, :]
-
-    rows = lax.broadcasted_iota(jnp.int32, (BLK, BLK), 0).astype(f32).astype(bf16)
-
-    def one_hot(index_row, b):
-        shifted = (index_row - b * BLK).astype(f32).astype(bf16)
-        hit = rows == jnp.broadcast_to(shifted, (BLK, BLK))
-        return jnp.where(hit, jnp.ones((), bf16), jnp.zeros((), bf16))
-
-    per_cell = op // BLK
-
-    @pl.loop(0, cells * per_cell)
-    def _(j):
-        at = pl.ds(pl.multiple_of(j * BLK, BLK), BLK)
-        index_row = idx[0:1, at]
-        got = jnp.zeros((width, BLK), f32)
-        for b in range(npad // BLK):
-            part = slice(b * BLK, (b + 1) * BLK)
-            block = one_hot(index_row, b)
-            hot[part, at] = block
-            got += jnp.dot(yb[:, part], block, preferred_element_type=f32)
-        row = pl.ds(pl.multiple_of(j // per_cell * width, width), width)
-        to = pl.ds(pl.multiple_of(j % per_cell * BLK, BLK), BLK)
-        vals[row, to] = got.astype(bf16)
-
-    slab_row = idx[0:1, jp + o_sl : jp + o_sl + 2 * flp].astype(f32)
-    slab_row = jnp.where(slab_row < 0, -2.0, slab_row)
-    for k in range(2 * fsp // 128):
-        row = idx[0:1, jp + k * 128 : jp + (k + 1) * 128].astype(f32)
-        col = jnp.broadcast_to(row, (128, 128)).T
-        cross[k * 128 : (k + 1) * 128, :] = jnp.where(col[:, 0:1] == slab_row, 1.0, 0.0).astype(bf16)
+    pl.loop(half, cells * per_cell)(build_gather)
 
     for copy in pack_copies:
         copy.wait()
@@ -203,15 +216,6 @@
         )
 
     for step in range(2):
-        if step > 0:
-            @pl.loop(0, cells * per_cell)
-            def _(j):
-                at = pl.ds(pl.multiple_of(j * BLK, BLK), BLK)
-                got = jnp.dot(yb[...], hot[:, at], preferred_element_type=f32)
-                row = pl.ds(pl.multiple_of(j // per_cell * width, width), width)
-                to = pl.ds(pl.multiple_of(j % per_cell * BLK, BLK), BLK)
-                vals[row, to] = got.astype(bf16)
-
         margin = jnp.zeros((width, lp), f32)
         for c in range(cells):
             margin += lax.dot_general(
@@ -256,36 +260,47 @@
             tot[0:width, cols] = high
             tot[width:, cols] = (total - high.astype(f32)).astype(bf16)
 
-        @pl.loop(0, npad // BLK)
+        @pl.loop(0, fp // BLK)
         def _(b):
+            to = pl.ds(pl.multiple_of(b * BLK, BLK), BLK)
+            both = lax.dot_general(tot[:, 0:jp], hote[to, :], NT, preferred_element_type=f32)
+            outg[step, :, to] = (both[0:width] + both[width:]).astype(bf16)
+
+        space_copies = [
+            face_copy(step, 0, fsp, in_space, {"space": above}),
+            face_copy(step, 1, 0, in_space, {"space": below}),
+        ]
+        for copy in space_copies:
+            copy.start()
+
+        def scatter(b, step=step):
             at = pl.ds(pl.multiple_of(b * BLK, BLK), BLK)
             if step == 0:
                 for j in range(fp // BLK):
                     hotf[at, j * BLK : (j + 1) * BLK] = one_hot(
                         idx[0:1, jp + j * BLK : jp + (j + 1) * BLK], b
                     )
-            both = lax.dot_general(tot[...], hot[at, :], NT, preferred_element_type=f32)
+            both = lax.dot_general(tot[:, 0:jp], hot[at, :], NT, preferred_element_type=f32)
             summed = both[0:width] + both[width:]
-            asm[:, at] = summed
-            asmb[:, at] = summed.astype(bf16)
-
-        @pl.loop(0, fp // BLK)
-        def _(b):
-            to = pl.ds(pl.multiple_of(b * BLK, BLK), BLK)
-            got = jnp.dot(asmb[...], hotf[:, to], preferred_element_type=f32)
-            outg[step, :, to] = got.astype(bf16)
-
-        space_copies = [
-            face_copy(step, 0, fsp, in_space, {"space": above}),
-            face_copy(step, 1, 0, in_space, {"space": below}),
-        ]
-        for copy in space_copies:
-            copy.start()
+            if step == 0:
+                start = yb[:, at].astype(f32)
+                partial = (summed - filter_centre * start) / filter_half
+                high = partial.astype(bf16)
+                zhl[0:width, at] = high
+                zhl[width:, at] = (partial - high.astype(f32)).astype(bf16)
+                asm2[:, at] = -2.0 * filter_centre * partial / filter_half - start
+            else:
+                asm2[:, at] += 2.0 * summed / filter_half
+
+        blocks = npad // BLK
+        first = blocks if step == 0 else blocks // 2
+        pl.loop(0, first)(scatter)
+
         for k, copy in enumerate(space_copies):
             copy.wait()
             part = slice(k * fsp, (k + 1) * fsp)
-            inc[:, part] = (in_space[step, k].astype(f32) * keep[:, part]).astype(bf16)
-        extra = jnp.dot(inc[:, 0:o_sl], cross[...], preferred_element_type=f32)
+            inc[step, :, part] = (in_space[step, k].astype(f32) * keep[:, part]).astype(bf16)
+        extra = jnp.dot(inc[step, :, 0:o_sl], cross[...], preferred_element_type=f32)
         part = slice(o_sl, o_sl + 2 * flp)
         outg[step, :, part] = (outg[step, :, part].astype(f32) + extra).astype(bf16)
         slab_copies = [
@@ -294,37 +309,50 @@
         ]
         for copy in slab_copies:
             copy.start()
+
+        if step == 0:
+            @pl.loop(0, cells * per_cell)
+            def _(j):
+                at = pl.ds(pl.multiple_of(j * BLK, BLK), BLK)
+                both = jnp.dot(zhl[...], hot[:, at], preferred_element_type=f32)
+                asm[:, at] = both[0:width] + both[width:]
+        else:
+            pl.loop(first, blocks)(scatter)
+
         for k, copy in enumerate(slab_copies):
             copy.wait()
             part = slice(o_sl + k * flp, o_sl + (k + 1) * flp)
-            inc[:, part] = (in_slab[step, k].astype(f32) * keep[:, part]).astype(bf16)
+            inc[step, :, part] = (in_slab[step, k].astype(f32) * keep[:, part]).astype(bf16)
 
         if step == 0:
-            @pl.loop(0, npad // BLK)
-            def _(b):
-                at = pl.ds(pl.multiple_of(b * BLK, BLK), BLK)
-                added = lax.dot_general(
-                    inc[...], hotf[at, :], NT, preferred_element_type=f32
-                )
-                start = yb[:, at].astype(f32)
-                current = (asm[:, at] + added - filter_centre * start) / filter_half
-                asm2[:, at] = -2.0 * filter_centre * current / filter_half - start
-                yb[:, at] = current.astype(bf16)
-        else:
-            def final(at):
-                added = lax.dot_general(
-                    inc[...], hotf[at, :], NT, preferred_element_type=f32
-                )
-                return 2.0 * (asm[:, at] + added) / filter_half + asm2[:, at]
-
-            @pl.loop(0, nodes // BLK)
-            def _(b):
-                at = pl.ds(pl.multiple_of(b * BLK, BLK), BLK)
-                out_ref[:, at] = final(at)
-
-            if nodes % BLK:
-                low = nodes // BLK * BLK
-                out_ref[:, low:nodes] = final(slice(low, low + BLK))[:, 0 : nodes - low]
+            @pl.loop(0, cells * per_cell)
+            def _(j):
+                at = pl.ds(pl.multiple_of(j * BLK, BLK), BLK)
+                added = jnp.dot(inc[0], hote[:, at], preferred_element_type=f32)
+                row = pl.ds(pl.multiple_of(j // per_cell * width, width), width)
+                to = pl.ds(pl.multiple_of(j % per_cell * BLK, BLK), BLK)
+                vals[row, to] = (asm[:, at] + added / filter_half).astype(bf16)
+
+    change = (
+        2.0 / filter_half * inc[1].astype(f32)
+        - 2.0 * filter_centre / filter_half / filter_half * inc[0].astype(f32)
+    )
+    high = change.astype(bf16)
+    tot[0:width, 0:fp] = high
+    tot[width:, 0:fp] = (change - high.astype(f32)).astype(bf16)
+
+    def final(at):
+        both = lax.dot_general(tot[:, 0:fp], hotf[at, :], NT, preferred_element_type=f32)
+        return asm2[:, at] + both[0:width] + both[width:]
+
+    @pl.loop(0, nodes // BLK)
+    def _(b):
+        at = pl.ds(pl.multiple_of(b * BLK, BLK), BLK)
+        out_ref[:, at] = final(at)
+
+    if nodes % BLK:
+        low = nodes // BLK * BLK
+        out_ref[:, low:nodes] = final(slice(low, low + BLK))[:, 0 : nodes - low]
 
 
 def shards(
@@ -368,24 +396,26 @@
         scratch_shapes=[
             pltpu.VMEM((npad, jp), bf16),
             pltpu.VMEM((npad, fp), bf16),
+            pltpu.VMEM((fp, jp), bf16),
             pltpu.VMEM((atoms * pstride + 8, lp), f32),
             pltpu.VMEM((8, jp + fp), jnp.int32),
             pltpu.VMEM((op, op), bf16),
             pltpu.VMEM((lp, jp), bf16),
             pltpu.VMEM((up(cells, 8), op), f32),
             pltpu.VMEM((2 * fsp, 2 * flp), bf16),
+            pltpu.VMEM((fp, 128), f32),
             pltpu.VMEM((others, atoms * pstride + 8, lp), f32),
             pltpu.VMEM((n_slab, lp, lp), f32),
             pltpu.VMEM((width, npad), bf16),
             pltpu.VMEM((cells * width, op), bf16),
-            pltpu.VMEM((2 * width, jp), bf16),
-            pltpu.VMEM((width, max(jp, npad)), f32),
-            pltpu.VMEM((width, npad), bf16),
+            pltpu.VMEM((2 * width, max(jp, fp)), bf16),
+            pltpu.VMEM((width, jp), f32),
+            pltpu.VMEM((2 * width, npad), bf16),
             pltpu.VMEM((width, npad), f32),
             pltpu.VMEM((2, width, fp), bf16),
             pltpu.VMEM((2, 2, width, fsp), bf16),
             pltpu.VMEM((2, 2, width, flp), bf16),
-            pltpu.VMEM((width, fp), bf16),
+            pltpu.VMEM((2, width, fp), bf16),
             pltpu.VMEM((2, n_slab, width, lp), f32),
             dma((others,)),
             dma((others,)),

time: 69.5 us -> 58.3 us (0.84)
  Pallas kernels: 67.3 us -> 56.1 us
    pallas_call x1, Pallas kernels: 67.3 us -> 56.1 us  [shards(): pl.pallas_call(functools.partial(kernel, dims), out_shape=jax.ShapeDtypeS...]
where the time goes in v3:
time: 58.3 us; the launch traced here: 58.1 us
  Pallas kernels  56.1 us (96%)
  local copies, waits for them, and re-layouts  1.99 us (3%)
    pallas_call x1, Pallas kernels, shards(): pl.pallas_call(functools.partial(kernel, dims), out_shape=jax.ShapeDtypeS...  56.1 us
    unnamed x1, local copies, waits for them, and re-layouts  1.99 us

profile of v3, /device:TPU:0, one launch (start us, length us, event | category | flops | bytes accessed | tf_op | source)
XLA Modules:
  0.0 58.1 jit_solution(15738533921986360705)
XLA Ops:
  0.0 56.1 %shard_map.100 = f32[64,2601]{1,0:T(8,128)} custom-call(bf16[64,2601]{1,0:T(8,128)(2,1)} %y_ref.1, bf16[729,729]{1,0:T(8,128)(2,1)} %kin_ref.1, f32[4]{0:T(128)} %scale_ref.1, f32[4,729]{1,0:T(4,128)} %pot_ref.1, s32[4,729]{1,0:T(4,128)} %cn_ref.1, s32[2,289]{1,0:T(2,128)} %fs_ref.1, s32[2,153]{1,0:T(2,128)} %fl_ref.1, bf16[18,4,729]{2,1,0:T(4,128)(2,1)} %bitcast.2, ...), custom_call_target="tpu_custom_call" | custom-call | tf_op jit(solution)/shard_map/pallas_call | solution.py:391
  56.1 2.0 %copy.12 = f32[64,2601]{1,0:T(8,128)} copy(f32[64,2601]{1,0:T(8,128)} %shard_map.100) | data formatting | bytes 1331712

commit v4 on v3

--- a/solution.py
+++ b/solution.py
@@ -36,6 +36,7 @@
     hot,
     hotf,
     hote,
+    dup,
     pack,
     idx,
     kin,
@@ -49,7 +50,8 @@
     vals,
     tot,
     asm,
-    zhl,
+    uhl,
+    first_total,
     asm2,
     outg,
     in_space,
@@ -157,8 +159,34 @@
                 part = slice(k * 128, (k + 1) * 128)
                 hote[part, lane] = jnp.where(fcol[part, :] == cell_row, 1.0, 0.0).astype(bf16)
 
+    n_pairs = cells * (cells - 1) // 2
+    hop = op // 2
+
+    def build_dup(u):
+        q, hf = u // 2, u % 2
+        one = q % cells
+        two = (one + 1 + q // cells) % cells
+        for k in range(hop // 128):
+            lane = pl.ds(pl.multiple_of(one * op + hf * hop + k * 128, 128), 128)
+            col = jnp.broadcast_to(idx[0:1, lane].astype(f32), (128, 128)).T
+            col = jnp.where(col < 0, -2.0, col)
+            to = pl.ds(pl.multiple_of(q * op + hf * hop + k * 128, 128), 128)
+            for h in range(op // 128):
+                lane = pl.ds(pl.multiple_of(two * op + h * 128, 128), 128)
+                row = jnp.broadcast_to(idx[0:1, lane].astype(f32), (128, 128))
+                dup[to, h * 128 : (h + 1) * 128] = jnp.where(col == row, 1.0, 0.0).astype(bf16)
+
+    together = 2 * n_pairs == cells * per_cell
+
+    def build_all(j):
+        build_gather(j)
+        if together:
+            build_dup(j)
+
+    if not together:
+        pl.loop(0, 2 * n_pairs)(build_dup)
     half = cells * per_cell // 2
-    pl.loop(0, half)(build_gather)
+    pl.loop(0, half)(build_all)
     pl.semaphore_wait(barrier, n_slab + 1)
     pack_copies = []
     for d in range(1, n_slab):
@@ -173,7 +201,7 @@
         copy.start()
         pack_copies.append(copy)
 
-    pl.loop(half, cells * per_cell)(build_gather)
+    pl.loop(half, cells * per_cell)(build_all)
 
     for copy in pack_copies:
         copy.wait()
@@ -259,6 +287,15 @@
             high = total.astype(bf16)
             tot[0:width, cols] = high
             tot[width:, cols] = (total - high.astype(f32)).astype(bf16)
+            if step == 0:
+                first_total[:, cols] = total
+            else:
+                step_change = 2.0 / filter_half * total - (
+                    2.0 * filter_centre / filter_half / filter_half * first_total[:, cols]
+                )
+                high = step_change.astype(bf16)
+                uhl[0:width, cols] = high
+                uhl[width:, cols] = (step_change - high.astype(f32)).astype(bf16)
 
         @pl.loop(0, fp // BLK)
         def _(b):
@@ -273,28 +310,50 @@
         for copy in space_copies:
             copy.start()
 
-        def scatter(b, step=step):
+        def scatter(b):
             at = pl.ds(pl.multiple_of(b * BLK, BLK), BLK)
-            if step == 0:
-                for j in range(fp // BLK):
-                    hotf[at, j * BLK : (j + 1) * BLK] = one_hot(
-                        idx[0:1, jp + j * BLK : jp + (j + 1) * BLK], b
-                    )
-            both = lax.dot_general(tot[:, 0:jp], hot[at, :], NT, preferred_element_type=f32)
-            summed = both[0:width] + both[width:]
-            if step == 0:
-                start = yb[:, at].astype(f32)
-                partial = (summed - filter_centre * start) / filter_half
-                high = partial.astype(bf16)
-                zhl[0:width, at] = high
-                zhl[width:, at] = (partial - high.astype(f32)).astype(bf16)
-                asm2[:, at] = -2.0 * filter_centre * partial / filter_half - start
-            else:
-                asm2[:, at] += 2.0 * summed / filter_half
+            for j in range(fp // BLK):
+                hotf[at, j * BLK : (j + 1) * BLK] = one_hot(
+                    idx[0:1, jp + j * BLK : jp + (j + 1) * BLK], b
+                )
+            both = lax.dot_general(uhl[...], hot[at, :], NT, preferred_element_type=f32)
+            start = yb[:, at].astype(f32)
+            kept = 2.0 * filter_centre * filter_centre / filter_half / filter_half - 1.0
+            asm2[:, at] = both[0:width] + both[width:] + kept * start
+
+        def share(c):
+            @pl.loop(0, per_cell)
+            def _(n):
+                to = pl.ds(pl.multiple_of(n * BLK, BLK), BLK)
+                both = jnp.zeros((2 * width, BLK), f32)
+                for q in range(n_pairs):
+                    one = q % cells
+                    two = (one + 1 + q // cells) % cells
+                    if two == c:
+                        both += jnp.dot(
+                            tot[:, one * op : (one + 1) * op],
+                            dup[q * op : (q + 1) * op, to],
+                            preferred_element_type=f32,
+                        )
+                    elif one == c:
+                        rows = pl.ds(pl.multiple_of(q * op + n * BLK, BLK), BLK)
+                        both += lax.dot_general(
+                            tot[:, two * op : (two + 1) * op],
+                            dup[rows, :],
+                            NT,
+                            preferred_element_type=f32,
+                        )
+                at = pl.ds(pl.multiple_of(c * op + n * BLK, BLK), BLK)
+                value = vals[c * width : (c + 1) * width, to].astype(f32)
+                summed = first_total[:, at] + both[0:width] + both[width:]
+                asm[:, at] = (summed - filter_centre * value) / filter_half
 
         blocks = npad // BLK
-        first = blocks if step == 0 else blocks // 2
-        pl.loop(0, first)(scatter)
+        if step == 0:
+            for c in range(cells // 2):
+                share(c)
+        else:
+            pl.loop(0, blocks // 2)(scatter)
 
         for k, copy in enumerate(space_copies):
             copy.wait()
@@ -311,13 +370,10 @@
             copy.start()
 
         if step == 0:
-            @pl.loop(0, cells * per_cell)
-            def _(j):
-                at = pl.ds(pl.multiple_of(j * BLK, BLK), BLK)
-                both = jnp.dot(zhl[...], hot[:, at], preferred_element_type=f32)
-                asm[:, at] = both[0:width] + both[width:]
+            for c in range(cells // 2, cells):
+                share(c)
         else:
-            pl.loop(first, blocks)(scatter)
+            pl.loop(blocks // 2, blocks)(scatter)
 
         for k, copy in enumerate(slab_copies):
             copy.wait()
@@ -397,6 +453,7 @@
             pltpu.VMEM((npad, jp), bf16),
             pltpu.VMEM((npad, fp), bf16),
             pltpu.VMEM((fp, jp), bf16),
+            pltpu.VMEM((cells * (cells - 1) // 2 * op, op), bf16),
             pltpu.VMEM((atoms * pstride + 8, lp), f32),
             pltpu.VMEM((8, jp + fp), jnp.int32),
             pltpu.VMEM((op, op), bf16),
@@ -410,7 +467,8 @@
             pltpu.VMEM((cells * width, op), bf16),
             pltpu.VMEM((2 * width, max(jp, fp)), bf16),
             pltpu.VMEM((width, jp), f32),
-            pltpu.VMEM((2 * width, npad), bf16),
+            pltpu.VMEM((2 * width, jp), bf16),
+            pltpu.VMEM((width, jp), f32),
             pltpu.VMEM((width, npad), f32),
             pltpu.VMEM((2, width, fp), bf16),
             pltpu.VMEM((2, 2, width, fsp), bf16),

time: 58.3 us -> 54.8 us (0.940)
  Pallas kernels: 56.1 us -> 52.6 us
    pallas_call x1, Pallas kernels: 56.1 us -> 52.6 us  [shards(): pl.pallas_call(functools.partial(kernel, dims), out_shape=jax.ShapeDtypeS...]
where the time goes in v4:
time: 54.8 us; the launch traced here: 54.6 us
  Pallas kernels  52.6 us (96%)
  local copies, waits for them, and re-layouts  1.99 us (4%)
    pallas_call x1, Pallas kernels, shards(): pl.pallas_call(functools.partial(kernel, dims), out_shape=jax.ShapeDtypeS...  52.6 us
    unnamed x1, local copies, waits for them, and re-layouts  1.99 us

profile of v4, /device:TPU:0, one launch (start us, length us, event | category | flops | bytes accessed | tf_op | source)
XLA Modules:
  0.0 54.6 jit_solution(12772348319676841682)
XLA Ops:
  0.0 52.6 %shard_map.100 = f32[64,2601]{1,0:T(8,128)} custom-call(bf16[64,2601]{1,0:T(8,128)(2,1)} %y_ref.1, bf16[729,729]{1,0:T(8,128)(2,1)} %kin_ref.1, f32[4]{0:T(128)} %scale_ref.1, f32[4,729]{1,0:T(4,128)} %pot_ref.1, s32[4,729]{1,0:T(4,128)} %cn_ref.1, s32[2,289]{1,0:T(2,128)} %fs_ref.1, s32[2,153]{1,0:T(2,128)} %fl_ref.1, bf16[18,4,729]{2,1,0:T(4,128)(2,1)} %bitcast.2, ...), custom_call_target="tpu_custom_call" | custom-call | tf_op jit(solution)/shard_map/pallas_call | solution.py:447
  52.6 2.0 %copy.12 = f32[64,2601]{1,0:T(8,128)} copy(f32[64,2601]{1,0:T(8,128)} %shard_map.100) | data formatting | bytes 1331712
